TPU v7x, 32 devices: a whole 2x2x4 slice. The times are simulated.
32 devices in a mesh: tm: 8 (over z, x), rows: 4 (over y, core).
Axes of the slice: x: 2, y: 2, z: 4, core: 2. Of those that a mesh axis runs over, the one named last changes fastest.
Arguments:
- clip: float32 [32, 8, 32, 128], P('tm', 'rows'), may hold values from -6 to 6
- kernel_one: float32 [3, 3, 3, 128, 128], replicated, may hold values from -0.109375 to 0.109375
- kernel_two: float32 [3, 3, 3, 128, 128], replicated, may hold values from -0.109375 to 0.109375
- cotangent: float32 [32, 8, 32, 128], P('tm', 'rows'), may hold values from -6 to 6
Outputs:
- block_out: float32 [32, 8, 32, 128], P('tm', 'rows')
- grad_clip: float32 [32, 8, 32, 128], P('tm', 'rows')
- grad_one: float32 [3, 3, 3, 128, 128], replicated
- grad_two: float32 [3, 3, 3, 128, 128], replicated
All inputs are finite; a program needn't handle non-finite values.
Results may differ from a plain program's by a relative error of at most 0.00014.
Values sent between devices are 32-bit elements; how exact they have to be, the bound alone decides.
No kernel may reach another device: no remote copies, remote signals or barrier semaphores. Data moves between devices by JAX's collectives and lax.ppermute only.
A program may use at most 128 MiB of HBM per device.

v0:
```python
import math
import jax
import jax.numpy as jnp
from jax import lax
from jax.sharding import PartitionSpec as P


def passed_along(value, axis, steps):
    count = lax.axis_size(axis)
    first, last = (max(0, -steps), min(count, count - steps))
    return lax.ppermute(value, axis, [(source, source + steps) for source in range(first, last)])


def padded_2(cells, sides, width):
    for axis, dim in sides:
        count = lax.axis_size(axis)
        ends = count - 1
        head = lax.slice_in_dim(cells, 0, width, axis=dim)
        tail = lax.slice_in_dim(cells, cells.shape[dim] - width, cells.shape[dim], axis=dim)
        cells = jnp.concatenate(
            [
                lax.ppermute(tail, axis, [(i, (i + 1) % count) for i in range(ends)]),
                cells,
                lax.ppermute(head, axis, [((i + 1) % count, i) for i in range(ends)]),
            ],
            axis=dim,
        )
    return cells


def columns(padded, step_time, step_row, out_frames, out_rows, span):
    window_piece = padded[step_time : step_time + out_frames, step_row : step_row + out_rows]
    joined = jnp.concatenate(
        [window_piece[:, :, offset : offset + span] for offset in range(3)], -1
    )
    return joined.reshape(out_frames * out_rows * span, -1)


def conv_local(extended, kernel):
    out_frames = extended.shape[0] - 2
    out_rows = extended.shape[1] - 2
    span = extended.shape[2]
    channels = extended.shape[3]
    padded = jnp.pad(extended, ((0, 0), (0, 0), (1, 1), (0, 0)))
    running = jnp.zeros((out_frames * out_rows * span, kernel.shape[-1]), jnp.float32)
    for step_time in range(3):
        for step_row in range(3):
            running = running + jnp.dot(
                columns(padded, step_time, step_row, out_frames, out_rows, span),
                kernel[step_time, step_row].reshape(3 * channels, -1),
                precision=lax.Precision.HIGHEST,
            )
    return running.reshape(out_frames, out_rows, span, -1)


def kernel_grad(extended, partner):
    out_frames = extended.shape[0] - 2
    out_rows = extended.shape[1] - 2
    span = extended.shape[2]
    channels = extended.shape[3]
    padded = jnp.pad(extended, ((0, 0), (0, 0), (1, 1), (0, 0)))
    flat_partner = partner.reshape(-1, partner.shape[-1])
    blocks = []
    for step_time in range(3):
        for step_row in range(3):
            product = lax.dot_general(
                columns(padded, step_time, step_row, out_frames, out_rows, span),
                flat_partner,
                (((0,), (0,)), ((), ())),
                precision=lax.Precision.HIGHEST,
            )
            blocks.append(product.reshape(3, channels, -1))
    return jnp.stack(blocks).reshape(3, 3, 3, channels, -1)


def flipped(kernel):
    return jnp.transpose(kernel[::-1, ::-1, ::-1], (0, 1, 2, 4, 3))


def frames_after(field):
    later = passed_along(field[:2], "tm", -1)
    return jnp.concatenate([field, later], 0)


def with_rims(field):
    return padded_2(field, (("rows", 1),), 1)


def per_device(clip, kernel_one, kernel_two, cotangent):
    frames, rows_here, span, channels = clip.shape
    height = rows_here * lax.axis_size("rows")
    factor = 1.0 / math.sqrt(frames * lax.axis_size("tm") * height * span)
    earlier = passed_along(clip, "tm", 1)
    deep_ext = padded_2(jnp.concatenate([earlier, clip], 0), (("rows", 1),), 2)
    pre_wide = conv_local(deep_ext, kernel_one)
    row_ids = lax.axis_index("rows") * rows_here - 1 + jnp.arange(rows_here + 2, dtype=jnp.int32)
    inside = ((row_ids >= 0) & (row_ids < height)).astype(jnp.float32)
    active_ext = jax.nn.silu(pre_wide) * inside[None, :, None, None]
    pre_one = pre_wide[2:, 1:-1]
    clip_ext = deep_ext[2:, 1:-1]
    block_out = clip + conv_local(active_ext, kernel_two)
    grad_ext = with_rims(frames_after(cotangent))
    d_active = conv_local(grad_ext, flipped(kernel_two))
    sigma = jax.nn.sigmoid(pre_one)
    delta = d_active * sigma * (1.0 + pre_one * (1.0 - sigma))
    grad_two = kernel_grad(active_ext, cotangent) * factor
    delta_ext = with_rims(frames_after(delta))
    grad_clip = cotangent + conv_local(delta_ext, flipped(kernel_one))
    grad_one = kernel_grad(clip_ext, delta) * factor
    grad_one, grad_two = lax.psum((grad_one, grad_two), ("tm", "rows"))
    return (block_out, grad_clip, grad_one, grad_two)


def solution(mesh):
    return jax.shard_map(
        per_device,
        mesh=mesh,
        in_specs=(P("tm", "rows", None, None), P(), P(), P("tm", "rows", None, None)),
        out_specs=(P("tm", "rows", None, None), P("tm", "rows", None, None), P(), P()),
        check_vma=False,
    )
```

profile of v0, /device:TPU:0, one launch (start us, length us, event | category | flops | bytes accessed | tf_op | source)
XLA Modules:
  0.0 273.9 jit_solution(3849822694402859812)
XLA Ops:
  7.2 5.5 %collective-permute-start = (f32[4,2,32,128]{3,2,1,0:T(8,128)}, f32[4,2,32,128]{3,2,1,0:T(8,128)}, u32[]{:S(2)}, u32[]{:S(2)}) collective-permute-start(f32[4,2,32,128]{3,2,1,0:T(8,128)} %param.4), channel_id=1, source_target_pairs={{0,4},{4,8},{8,12},{12,16},{16,20},{20,24},{24,28},{1,5},{5,9},{9,... | collective-permute-start | bytes 393224 | tf_op jit(solution)/shard_map/ppermute | solution.py:11
  12.7 1.5 slice.904
  14.2 1.3 collective-permute-start.3
  15.5 1.6 constant_dynamic-update-slice_fusion.3
  17.1 2.8 %fusion.48 = (f32[1,1,3,128,128]{4,3,2,1,0:T(8,128)}, f32[1,1,3,128,128]{4,3,2,1,0:T(8,128)}, f32[1,1,3,128,128]{4,3,2,1,0:T(8,128)}, f32[1,1,3,128,128]{4,3,2,1...) fusion(f32[3,3,3,128,128]{4,3,2,1,0:T(8,128)} %param.6), kind=kLoop, calls=%fused_computation.252 | loop fusion | bytes 3538944 | tf_op jit(solution)/shard_map/slice | solution.py:50
  19.9 2.0 copy.26
  21.9 1.2 fusion.49
  23.1 1.5 copy.27
  24.7 1.7 reverse_bitcast_fusion.1
  26.6 1.3 fusion.46
  28.8 1.3 collective-permute-start.5
  30.1 3.0 %collective-permute-start.4 = (f32[6,1,32,128]{3,2,1,0:T(8,128)S(1)}, f32[6,1,32,128]{3,2,1,0:T(8,128)S(1)}, u32[]{:S(2)}, u32[]{:S(2)}) collective-permute-start(f32[6,1,32,128]{3,2,1,0:T(8,128)S(1)} %get-tuple-element.185), channel_id=1, source_target_pairs={{0,1},{1,2},{2,3},{4,5},{5,6},{6,7},{8,9},{9,10},{10,11},{12,13},{... | collective-permute-start | bytes 294920 | tf_op jit(solution)/shard_map/ppermute | solution.py:22
  34.1 1.3 collective-permute-start.2
  35.4 4.1 %collective-permute-start.1 = (f32[8,2,32,128]{3,2,1,0:T(8,128)S(1)}, f32[8,2,32,128]{3,2,1,0:T(8,128)S(1)}, u32[]{:S(2)}, u32[]{:S(2)}) collective-permute-start(f32[8,2,32,128]{3,2,1,0:T(8,128)S(1)} %constant_dynamic-update-slice_fusion), channel_id=1, source_target_pairs={{0,1},{1,2},{2,3},{4,5},{5,6},{6,7},{8,9},{9,10},{10,11},{12,13},{... | collective-permute-start | bytes 786440 | tf_op jit(solution)/shard_map/ppermute | solution.py:22
  48.4 1.2 convolution_add_fusion.7
  50.5 1.2 convolution_add_fusion.6
  51.7 1.2 convolution_add_fusion.5
  53.8 14.2 %convolution_add_fusion.4 = f32[768,128]{1,0:T(8,128)S(1)} fusion(f32[768,128]{1,0:T(8,128)S(1)} %convolution_add_fusion.5, f32[768,384]{1,0:T(8,128)S(1)} %bitcast.357, f32[384,128]{1,0:T(8,128)S(1)} %bitcast.429), kind=kOutput, calls=%fused_computation.24 | convolution fusion | flops 453083136 | bytes 2162688 | tf_op jit(solution)/shard_map/dot_general | solution.py:48
  68.0 1.2 convolution_add_fusion.3
  74.6 1.4 pad_slice_fusion.57
  77.0 1.3 pad_slice_fusion.39
  80.5 1.4 collective-permute-start.6
  87.3 1.3 pad_maximum_fusion.44
  95.4 1.4 broadcast_multiply_fusion.1
  105.8 1.5 fusion.8
  107.3 1.5 fusion.7
  112.4 1.6 broadcast_multiply_fusion
  118.7 1.3 collective-permute-start.8
  120.0 4.3 %collective-permute-start.7 = (f32[6,1,32,128]{3,2,1,0:T(8,128)S(1)}, f32[6,1,32,128]{3,2,1,0:T(8,128)S(1)}, u32[]{:S(2)}, u32[]{:S(2)}) collective-permute-start(f32[6,1,32,128]{3,2,1,0:T(8,128)S(1)} %get-tuple-element.175), channel_id=1, source_target_pairs={{0,1},{1,2},{2,3},{4,5},{5,6},{6,7},{8,9},{9,10},{10,11},{12,13},{... | collective-permute-start | bytes 294920 | tf_op jit(solution)/shard_map/ppermute | solution.py:22
  132.7 129.8 %all-reduce.8.cloned.1.call-done = (f32[3,3,3,128,128]{4,3,2,1,0:T(8,128)}, f32[3,3,3,128,128]{4,3,2,1,0:T(8,128)}) async-done(((f32[3,3,3,128,128]{4,3,2,1,0:T(8,128)}, f32[3,3,3,128,128]{4,3,2,1,0:T(8,128)}), (f32[3,3,3,128,128]{4,3,2,1,0:T(8,128)}, f32[3,3,3,128,128]{4,3,2,1,0:T(8,128)})) %all-reduce.8.cloned.1.call-update) | async-done | bytes 3538960 | tf_op jit(solution)/shard_map/psum | solution.py:110
  262.6 3.0 %copy.66 = f32[3,3,3,128,128]{4,3,2,1,0:T(8,128)} copy(f32[3,3,3,128,128]{4,3,2,1,0:T(8,128)} %get-tuple-element.213) | data formatting | bytes 3538944
  265.6 1.2 copy.67
  (281 shorter events, 58.0 us)
Async XLA Ops:
  7.2 255.4 %all-reduce.8.cloned.1.call-start = ((), (), s32[]{:S(2)}) async-start(), calls=%async_computation | async-start | bytes 7077888 | tf_op jit(solution)/shard_map/psum | solution.py:110
  7.2 25.9 %collective-permute-start = (f32[4,2,32,128]{3,2,1,0:T(8,128)}, f32[4,2,32,128]{3,2,1,0:T(8,128)}, u32[]{:S(2)}, u32[]{:S(2)}) collective-permute-start(f32[4,2,32,128]{3,2,1,0:T(8,128)} %param.4), channel_id=1, source_target_pairs={{0,4},{4,8},{8,12},{12,16},{16,20},{20,24},{24,28},{1,5},{5,9},{9,... | collective-permute-start | bytes 393224 | tf_op jit(solution)/shard_map/ppermute | solution.py:11
  14.2 13.7 %collective-permute-start.3 = (f32[2,2,32,128]{3,2,1,0:T(8,128)}, f32[2,2,32,128]{3,2,1,0:T(8,128)}, u32[]{:S(2)}, u32[]{:S(2)}) collective-permute-start(f32[2,2,32,128]{3,2,1,0:T(8,128)} %slice.904), channel_id=1, source_target_pairs={{4,0},{8,4},{12,8},{16,12},{20,16},{24,20},{28,24},{5,1},{9,5},{13... | collective-permute-start | bytes 196616 | tf_op jit(solution)/shard_map/ppermute | solution.py:11
  17.1 2.9 %copy-start.1 = (f32[3,3,3,128,128]{4,3,2,1,0:T(8,128)S(1)}, f32[3,3,3,128,128]{4,3,2,1,0:T(8,128)}, u32[]{:S(2)}) copy-start(f32[3,3,3,128,128]{4,3,2,1,0:T(8,128)} %param.6) | copy-start | bytes 5308420
  19.9 2.0 copy-start.2
  26.6 7.4 %copy-start.13 = (f32[4,2,32,128]{3,2,1,0:T(8,128)S(1)}, f32[4,2,32,128]{3,2,1,0:T(8,128)}, u32[]{:S(2)}) copy-start(f32[4,2,32,128]{3,2,1,0:T(8,128)} %param.4) | copy-start | bytes 393220
  28.8 10.7 %collective-permute-start.5 = (f32[6,1,32,128]{3,2,1,0:T(8,128)S(1)}, f32[6,1,32,128]{3,2,1,0:T(8,128)S(1)}, u32[]{:S(2)}, u32[]{:S(2)}) collective-permute-start(f32[6,1,32,128]{3,2,1,0:T(8,128)S(1)} %get-tuple-element.186), channel_id=1, source_target_pairs={{1,0},{2,1},{3,2},{5,4},{6,5},{7,6},{9,8},{10,9},{11,10},{13,12},{... | collective-permute-start | bytes 294920 | tf_op jit(solution)/shard_map/ppermute | solution.py:24
  30.1 9.4 %collective-permute-start.4 = (f32[6,1,32,128]{3,2,1,0:T(8,128)S(1)}, f32[6,1,32,128]{3,2,1,0:T(8,128)S(1)}, u32[]{:S(2)}, u32[]{:S(2)}) collective-permute-start(f32[6,1,32,128]{3,2,1,0:T(8,128)S(1)} %get-tuple-element.185), channel_id=1, source_target_pairs={{0,1},{1,2},{2,3},{4,5},{5,6},{6,7},{8,9},{9,10},{10,11},{12,13},{... | collective-permute-start | bytes 294920 | tf_op jit(solution)/shard_map/ppermute | solution.py:22
  34.1 10.7 %collective-permute-start.2 = (f32[8,2,32,128]{3,2,1,0:T(8,128)S(1)}, f32[8,2,32,128]{3,2,1,0:T(8,128)S(1)}, u32[]{:S(2)}, u32[]{:S(2)}) collective-permute-start(f32[8,2,32,128]{3,2,1,0:T(8,128)S(1)} %constant_dynamic-update-slice_fusion), channel_id=1, source_target_pairs={{1,0},{2,1},{3,2},{5,4},{6,5},{7,6},{9,8},{10,9},{11,10},{13,12},{... | collective-permute-start | bytes 786440 | tf_op jit(solution)/shard_map/ppermute | solution.py:24
  35.4 9.4 %collective-permute-start.1 = (f32[8,2,32,128]{3,2,1,0:T(8,128)S(1)}, f32[8,2,32,128]{3,2,1,0:T(8,128)S(1)}, u32[]{:S(2)}, u32[]{:S(2)}) collective-permute-start(f32[8,2,32,128]{3,2,1,0:T(8,128)S(1)} %constant_dynamic-update-slice_fusion), channel_id=1, source_target_pairs={{0,1},{1,2},{2,3},{4,5},{5,6},{6,7},{8,9},{9,10},{10,11},{12,13},{... | collective-permute-start | bytes 786440 | tf_op jit(solution)/shard_map/ppermute | solution.py:22
  53.2 14.9 %copy-start.18 = (f32[1,1,3,128,128]{4,3,2,1,0:T(8,128)S(1)}, f32[1,1,3,128,128]{4,3,2,1,0:T(8,128)}, u32[]{:S(2)}) copy-start(f32[1,1,3,128,128]{4,3,2,1,0:T(8,128)} %get-tuple-element.36) | copy-start | bytes 589828
  80.4 2.4 copy-start.68
  80.4 2.4 copy-start.69
  80.4 2.4 copy-start.70
  80.4 2.4 copy-start.71
  80.4 2.4 copy-start.72
  80.4 2.4 copy-start.73
  80.5 38.1 %collective-permute-start.6 = (f32[2,2,32,128]{3,2,1,0:T(8,128)S(1)}, f32[2,2,32,128]{3,2,1,0:T(8,128)S(1)}, u32[]{:S(2)}, u32[]{:S(2)}) collective-permute-start(f32[2,2,32,128]{3,2,1,0:T(8,128)S(1)} %slice.1071), channel_id=1, source_target_pairs={{4,0},{8,4},{12,8},{16,12},{20,16},{24,20},{28,24},{5,1},{9,5},{13... | collective-permute-start | bytes 196616 | tf_op jit(solution)/shard_map/ppermute | solution.py:11
  97.9 2.0 copy-start.51
  97.9 2.0 copy-start.52
  98.9 2.0 copy-start.49
  98.9 2.0 copy-start.50
  98.9 2.0 copy-start.60
  99.9 2.0 copy-start.47
  99.9 2.0 copy-start.48
  105.8 3.1 %copy-start.5 = (f32[256,384]{0,1:T(8,128)S(1)}, f32[256,384]{0,1:T(8,128)}, u32[]{:S(2)}) copy-start(f32[256,384]{0,1:T(8,128)} %copy.39) | copy-start | bytes 1179652
  105.8 3.6 %copy-start.6 = (f32[256,384]{0,1:T(8,128)S(1)}, f32[256,384]{0,1:T(8,128)}, u32[]{:S(2)}) copy-start(f32[256,384]{0,1:T(8,128)} %copy.40) | copy-start | bytes 1179652
  107.3 2.6 copy-start.7
  112.4 2.1 copy-start.40
  118.7 5.6 %collective-permute-start.8 = (f32[6,1,32,128]{3,2,1,0:T(8,128)S(1)}, f32[6,1,32,128]{3,2,1,0:T(8,128)S(1)}, u32[]{:S(2)}, u32[]{:S(2)}) collective-permute-start(f32[6,1,32,128]{3,2,1,0:T(8,128)S(1)} %get-tuple-element.176), channel_id=1, source_target_pairs={{1,0},{2,1},{3,2},{5,4},{6,5},{7,6},{9,8},{10,9},{11,10},{13,12},{... | collective-permute-start | bytes 294920 | tf_op jit(solution)/shard_map/ppermute | solution.py:24
  120.0 5.2 %collective-permute-start.7 = (f32[6,1,32,128]{3,2,1,0:T(8,128)S(1)}, f32[6,1,32,128]{3,2,1,0:T(8,128)S(1)}, u32[]{:S(2)}, u32[]{:S(2)}) collective-permute-start(f32[6,1,32,128]{3,2,1,0:T(8,128)S(1)} %get-tuple-element.175), channel_id=1, source_target_pairs={{0,1},{1,2},{2,3},{4,5},{5,6},{6,7},{8,9},{9,10},{10,11},{12,13},{... | collective-permute-start | bytes 294920 | tf_op jit(solution)/shard_map/ppermute | solution.py:22
  262.6 3.0 %copy-start.4 = (f32[3,3,3,128,128]{4,3,2,1,0:T(8,128)S(1)}, f32[3,3,3,128,128]{4,3,2,1,0:T(8,128)}, u32[]{:S(2)}) copy-start(f32[3,3,3,128,128]{4,3,2,1,0:T(8,128)} %get-tuple-element.214) | copy-start | bytes 5308420
  (52 other events, 73.4 us)
Sparse Core Ops, SparseCore 0:
  118.8 143.7 all-reduce.7
where the time goes:
time: 277 us; the launch traced here: 274 us
  waiting for transfers between devices  131 us (47%)
  matrix products  47.7 us (17%)
  local copies, waits for them, and re-layouts  43.1 us (16%)
  starting transfers between devices  23.5 us (8%)
  between operations  15.8 us (6%)
  other arithmetic  13 us (5%)
    psum x1, waiting for transfers between devices, per_device(): grad_one, grad_two = lax.psum((grad_one, grad_two), ('tm', 'rows'))  130 us
    dot_general x36, matrix products, conv_local(): jnp.dot(columns(padded, step_time, step_row, out_frames, out_rows, span),...  37 us
    unnamed x154, local copies, waits for them, and re-layouts  16.7 us
    reshape x18, local copies, waits for them, and re-layouts, columns(): return joined.reshape(out_frames * out_rows * span, -1)  11.5 us
    ppermute x3, starting transfers between devices, padded_2(): lax.ppermute(tail, axis, [(i, (i + 1) % count) for i in range(ends)])  11.3 us
    dot_general x18, matrix products, kernel_grad(): lax.dot_general(columns(padded, step_time, step_row, out_frames, out_rows...  10.7 us
    ppermute x3, starting transfers between devices, passed_along(): lax.ppermute(value, axis, [(source, source + steps) for source in range(f...  8.24 us
    concatenate x30, other arithmetic, columns(): jnp.concatenate([window_piece[:, :, offset:offset + span] for offset in r...  6.96 us
  transfers between devices with their start and end apart: 10, of which 2 were waited for; matrix products, arithmetic and copies ran while one was open for 22% of the time, Pallas kernels for 0%

commit v1 on v0

--- a/solution.py
+++ b/solution.py
@@ -3,6 +3,11 @@
 import jax.numpy as jnp
 from jax import lax
 from jax.sharding import PartitionSpec as P
+
+
+def axis_by_axis(x, inner_axis, outer_axis):
+    inner = lax.psum(x, inner_axis)
+    return lax.psum(inner, outer_axis)
 
 
 def passed_along(value, axis, steps):
@@ -107,7 +112,7 @@
     delta_ext = with_rims(frames_after(delta))
     grad_clip = cotangent + conv_local(delta_ext, flipped(kernel_one))
     grad_one = kernel_grad(clip_ext, delta) * factor
-    grad_one, grad_two = lax.psum((grad_one, grad_two), ("tm", "rows"))
+    grad_one, grad_two = axis_by_axis((grad_one, grad_two), "rows", "tm")
     return (block_out, grad_clip, grad_one, grad_two)
 
 

time: 277 us -> 354 us (1.28)
  waiting for transfers between devices: 131 us -> 204 us
    psum x1 -> x2, waiting for transfers between devices: 130 us -> 204 us  [the longest x1 135 us: axis_by_axis(): return lax.psum(inner, outer_axis)]
    unnamed x154 -> x162, local copies, waits for them, and re-layouts: 16.7 us -> 15.9 us
  transfers between devices with their start and end apart: 10 -> 11, of which waited for: 2 -> 3; matrix products, arithmetic and copies ran while one was open for 22% -> 19% of each run, Pallas kernels for 0% -> 0%
where the time goes in v1:
time: 354 us; the launch traced here: 351 us
  waiting for transfers between devices  204 us (58%)
  matrix products  49.4 us (14%)
  local copies, waits for them, and re-layouts  43.1 us (12%)
  starting transfers between devices  23.4 us (7%)
  between operations  15.8 us (4%)
  other arithmetic  15.4 us (4%)
    psum x1, waiting for transfers between devices, axis_by_axis(): return lax.psum(inner, outer_axis)  135 us
    psum x1, waiting for transfers between devices, axis_by_axis(): inner = lax.psum(x, inner_axis)  68.3 us
    dot_general x36, matrix products, conv_local(): jnp.dot(columns(padded, step_time, step_row, out_frames, out_rows, span),...  37.6 us
    unnamed x162, local copies, waits for them, and re-layouts  15.9 us
    dot_general x18, matrix products, kernel_grad(): lax.dot_general(columns(padded, step_time, step_row, out_frames, out_rows...  11.8 us
    reshape x18, local copies, waits for them, and re-layouts, columns(): return joined.reshape(out_frames * out_rows * span, -1)  11.6 us
    ppermute x3, starting transfers between devices, padded_2(): lax.ppermute(tail, axis, [(i, (i + 1) % count) for i in range(ends)])  11.4 us
    concatenate x30, other arithmetic, columns(): jnp.concatenate([window_piece[:, :, offset:offset + span] for offset in r...  8.87 us
  transfers between devices with their start and end apart: 11, of which 3 were waited for; matrix products, arithmetic and copies ran while one was open for 19% of the time, Pallas kernels for 0%

profile of v1, /device:TPU:0, one launch (start us, length us, event | category | flops | bytes accessed | tf_op | source)
XLA Modules:
  0.0 351.1 jit_solution(16741174536551765278)
XLA Ops:
  7.2 5.5 %collective-permute-start = (f32[4,2,32,128]{3,2,1,0:T(8,128)}, f32[4,2,32,128]{3,2,1,0:T(8,128)}, u32[]{:S(2)}, u32[]{:S(2)}) collective-permute-start(f32[4,2,32,128]{3,2,1,0:T(8,128)} %param.4), channel_id=1, source_target_pairs={{0,4},{4,8},{8,12},{12,16},{16,20},{20,24},{24,28},{1,5},{5,9},{9,... | collective-permute-start | bytes 393224 | tf_op jit(solution)/shard_map/ppermute | solution.py:16
  12.7 1.5 slice.904
  14.2 1.3 collective-permute-start.3
  15.5 1.6 constant_dynamic-update-slice_fusion.3
  17.1 2.9 fusion.48
  20.0 2.0 copy.26
  22.0 1.2 fusion.49
  23.2 1.5 copy.27
  24.7 1.7 reverse_bitcast_fusion.1
  26.7 1.3 fusion.46
  28.8 1.3 collective-permute-start.5
  30.1 3.0 collective-permute-start.4
  34.1 1.3 collective-permute-start.2
  35.4 4.1 %collective-permute-start.1 = (f32[8,2,32,128]{3,2,1,0:T(8,128)S(1)}, f32[8,2,32,128]{3,2,1,0:T(8,128)S(1)}, u32[]{:S(2)}, u32[]{:S(2)}) collective-permute-start(f32[8,2,32,128]{3,2,1,0:T(8,128)S(1)} %constant_dynamic-update-slice_fusion), channel_id=1, source_target_pairs={{0,1},{1,2},{2,3},{4,5},{5,6},{6,7},{8,9},{9,10},{10,11},{12,13},{... | collective-permute-start | bytes 786440 | tf_op jit(solution)/shard_map/ppermute | solution.py:27
  51.8 1.2 convolution_add_fusion.5
  53.9 14.2 %convolution_add_fusion.4 = f32[768,128]{1,0:T(8,128)S(1)} fusion(f32[768,128]{1,0:T(8,128)S(1)} %convolution_add_fusion.5, f32[768,384]{1,0:T(8,128)S(1)} %bitcast.357, f32[384,128]{1,0:T(8,128)S(1)} %bitcast.429), kind=kOutput, calls=%fused_computation.24 | convolution fusion | flops 453083136 | bytes 2162688 | tf_op jit(solution)/shard_map/dot_general | solution.py:53
  68.1 1.2 convolution_add_fusion.3
  73.9 1.4 pad_slice_fusion.57
  76.3 1.3 pad_slice_fusion.39
  79.8 1.3 collective-permute-start.6
  85.9 1.3 pad_maximum_fusion.44
  94.0 1.4 broadcast_multiply_fusion.1
  106.1 1.6 fusion.8
  107.7 1.5 fusion.7
  109.2 1.5 fusion.6
  113.8 1.4 broadcast_multiply_fusion
  121.5 1.3 collective-permute-start.8
  122.8 4.3 %collective-permute-start.7 = (f32[6,1,32,128]{3,2,1,0:T(8,128)S(1)}, f32[6,1,32,128]{3,2,1,0:T(8,128)S(1)}, u32[]{:S(2)}, u32[]{:S(2)}) collective-permute-start(f32[6,1,32,128]{3,2,1,0:T(8,128)S(1)} %get-tuple-element.177), channel_id=1, source_target_pairs={{0,1},{1,2},{2,3},{4,5},{5,6},{6,7},{8,9},{9,10},{10,11},{12,13},{... | collective-permute-start | bytes 294920 | tf_op jit(solution)/shard_map/ppermute | solution.py:27
  129.1 68.3 %all-reduce.12.cloned.1.call-done = (f32[3,3,3,128,128]{4,3,2,1,0:T(8,128)}, f32[3,3,3,128,128]{4,3,2,1,0:T(8,128)}) async-done(((f32[3,3,3,128,128]{4,3,2,1,0:T(8,128)}, f32[3,3,3,128,128]{4,3,2,1,0:T(8,128)}), (f32[3,3,3,128,128]{4,3,2,1,0:T(8,128)}, f32[3,3,3,128,128]{4,3,2,1,0:T(8,128)})) %all-reduce.12.cloned.1.call-update) | async-done | bytes 3538960 | tf_op jit(solution)/shard_map/psum | solution.py:9
  204.5 135.4 %all-reduce.10.cloned.1.call-done = (f32[3,3,3,128,128]{4,3,2,1,0:T(8,128)}, f32[3,3,3,128,128]{4,3,2,1,0:T(8,128)}) async-done(((f32[3,3,3,128,128]{4,3,2,1,0:T(8,128)}, f32[3,3,3,128,128]{4,3,2,1,0:T(8,128)}), (f32[3,3,3,128,128]{4,3,2,1,0:T(8,128)}, f32[3,3,3,128,128]{4,3,2,1,0:T(8,128)})) %all-reduce.10.cloned.1.call-update) | async-done | bytes 3538960 | tf_op jit(solution)/shard_map/psum | solution.py:10
  339.8 3.0 copy.68
  342.8 1.2 copy.69
  (292 shorter events, 62.5 us)
Async XLA Ops:
  7.2 190.2 %all-reduce.12.cloned.1.call-start = ((), (), s32[]{:S(2)}) async-start(), calls=%async_computation.1 | async-start | bytes 7077888 | tf_op jit(solution)/shard_map/psum | solution.py:9
  7.2 26.0 %collective-permute-start = (f32[4,2,32,128]{3,2,1,0:T(8,128)}, f32[4,2,32,128]{3,2,1,0:T(8,128)}, u32[]{:S(2)}, u32[]{:S(2)}) collective-permute-start(f32[4,2,32,128]{3,2,1,0:T(8,128)} %param.4), channel_id=1, source_target_pairs={{0,4},{4,8},{8,12},{12,16},{16,20},{20,24},{24,28},{1,5},{5,9},{9,... | collective-permute-start | bytes 393224 | tf_op jit(solution)/shard_map/ppermute | solution.py:16
  14.2 13.7 %collective-permute-start.3 = (f32[2,2,32,128]{3,2,1,0:T(8,128)}, f32[2,2,32,128]{3,2,1,0:T(8,128)}, u32[]{:S(2)}, u32[]{:S(2)}) collective-permute-start(f32[2,2,32,128]{3,2,1,0:T(8,128)} %slice.904), channel_id=1, source_target_pairs={{4,0},{8,4},{12,8},{16,12},{20,16},{24,20},{28,24},{5,1},{9,5},{13... | collective-permute-start | bytes 196616 | tf_op jit(solution)/shard_map/ppermute | solution.py:16
  17.1 2.9 copy-start.1
  26.7 7.5 %copy-start.12 = (f32[4,2,32,128]{3,2,1,0:T(8,128)S(1)}, f32[4,2,32,128]{3,2,1,0:T(8,128)}, u32[]{:S(2)}) copy-start(f32[4,2,32,128]{3,2,1,0:T(8,128)} %param.4) | copy-start | bytes 393220
  28.8 10.7 %collective-permute-start.5 = (f32[6,1,32,128]{3,2,1,0:T(8,128)S(1)}, f32[6,1,32,128]{3,2,1,0:T(8,128)S(1)}, u32[]{:S(2)}, u32[]{:S(2)}) collective-permute-start(f32[6,1,32,128]{3,2,1,0:T(8,128)S(1)} %get-tuple-element.188), channel_id=1, source_target_pairs={{1,0},{2,1},{3,2},{5,4},{6,5},{7,6},{9,8},{10,9},{11,10},{13,12},{... | collective-permute-start | bytes 294920 | tf_op jit(solution)/shard_map/ppermute | solution.py:29
  30.1 9.4 %collective-permute-start.4 = (f32[6,1,32,128]{3,2,1,0:T(8,128)S(1)}, f32[6,1,32,128]{3,2,1,0:T(8,128)S(1)}, u32[]{:S(2)}, u32[]{:S(2)}) collective-permute-start(f32[6,1,32,128]{3,2,1,0:T(8,128)S(1)} %get-tuple-element.187), channel_id=1, source_target_pairs={{0,1},{1,2},{2,3},{4,5},{5,6},{6,7},{8,9},{9,10},{10,11},{12,13},{... | collective-permute-start | bytes 294920 | tf_op jit(solution)/shard_map/ppermute | solution.py:27
  34.1 10.7 %collective-permute-start.2 = (f32[8,2,32,128]{3,2,1,0:T(8,128)S(1)}, f32[8,2,32,128]{3,2,1,0:T(8,128)S(1)}, u32[]{:S(2)}, u32[]{:S(2)}) collective-permute-start(f32[8,2,32,128]{3,2,1,0:T(8,128)S(1)} %constant_dynamic-update-slice_fusion), channel_id=1, source_target_pairs={{1,0},{2,1},{3,2},{5,4},{6,5},{7,6},{9,8},{10,9},{11,10},{13,12},{... | collective-permute-start | bytes 786440 | tf_op jit(solution)/shard_map/ppermute | solution.py:29
  35.4 9.4 %collective-permute-start.1 = (f32[8,2,32,128]{3,2,1,0:T(8,128)S(1)}, f32[8,2,32,128]{3,2,1,0:T(8,128)S(1)}, u32[]{:S(2)}, u32[]{:S(2)}) collective-permute-start(f32[8,2,32,128]{3,2,1,0:T(8,128)S(1)} %constant_dynamic-update-slice_fusion), channel_id=1, source_target_pairs={{0,1},{1,2},{2,3},{4,5},{5,6},{6,7},{8,9},{9,10},{10,11},{12,13},{... | collective-permute-start | bytes 786440 | tf_op jit(solution)/shard_map/ppermute | solution.py:27
  53.2 14.9 %copy-start.17 = (f32[1,1,3,128,128]{4,3,2,1,0:T(8,128)S(1)}, f32[1,1,3,128,128]{4,3,2,1,0:T(8,128)}, u32[]{:S(2)}) copy-start(f32[1,1,3,128,128]{4,3,2,1,0:T(8,128)} %get-tuple-element.38) | copy-start | bytes 589828
  78.6 3.4 copy-start.72
  78.6 3.4 copy-start.73
  78.6 3.4 copy-start.74
  78.6 3.4 copy-start.75
  78.6 3.4 copy-start.76
  78.6 3.4 copy-start.77
  79.8 41.6 %collective-permute-start.6 = (f32[2,2,32,128]{3,2,1,0:T(8,128)S(1)}, f32[2,2,32,128]{3,2,1,0:T(8,128)S(1)}, u32[]{:S(2)}, u32[]{:S(2)}) collective-permute-start(f32[2,2,32,128]{3,2,1,0:T(8,128)S(1)} %slice.1071), channel_id=1, source_target_pairs={{4,0},{8,4},{12,8},{16,12},{20,16},{24,20},{28,24},{5,1},{9,5},{13... | collective-permute-start | bytes 196616 | tf_op jit(solution)/shard_map/ppermute | solution.py:16
  98.4 2.9 copy-start.50
  98.4 2.9 copy-start.51
  99.4 3.8 %copy-start.47 = (f32[4,2,32,128]{3,2,1,0:T(8,128)S(1)}, f32[4,2,32,128]{3,2,1,0:T(8,128)}, u32[]{:S(2)}) copy-start(f32[4,2,32,128]{3,2,1,0:T(8,128)} %get-tuple-element.143) | copy-start | bytes 393220
  99.4 3.8 %copy-start.48 = (f32[4,2,32,128]{3,2,1,0:T(8,128)S(1)}, f32[4,2,32,128]{3,2,1,0:T(8,128)}, u32[]{:S(2)}) copy-start(f32[4,2,32,128]{3,2,1,0:T(8,128)} %get-tuple-element.144) | copy-start | bytes 393220
  99.4 3.8 %copy-start.49 = (f32[4,2,32,128]{3,2,1,0:T(8,128)S(1)}, f32[4,2,32,128]{3,2,1,0:T(8,128)}, u32[]{:S(2)}) copy-start(f32[4,2,32,128]{3,2,1,0:T(8,128)} %get-tuple-element.147) | copy-start | bytes 393220
  106.1 4.7 %copy-start.5 = (f32[256,384]{0,1:T(8,128)S(1)}, f32[256,384]{0,1:T(8,128)}, u32[]{:S(2)}) copy-start(f32[256,384]{0,1:T(8,128)} %copy.40) | copy-start | bytes 1179652
  106.1 5.2 %copy-start.6 = (f32[256,384]{0,1:T(8,128)S(1)}, f32[256,384]{0,1:T(8,128)}, u32[]{:S(2)}) copy-start(f32[256,384]{0,1:T(8,128)} %copy.41) | copy-start | bytes 1179652
  106.1 5.7 %copy-start.7 = (f32[256,384]{0,1:T(8,128)S(1)}, f32[256,384]{0,1:T(8,128)}, u32[]{:S(2)}) copy-start(f32[256,384]{0,1:T(8,128)} %copy.42) | copy-start | bytes 1179652
  107.7 4.6 %copy-start.8 = (f32[256,384]{0,1:T(8,128)S(1)}, f32[256,384]{0,1:T(8,128)}, u32[]{:S(2)}) copy-start(f32[256,384]{0,1:T(8,128)} %copy.43) | copy-start | bytes 1179652
  109.2 3.5 %copy-start.9 = (f32[256,384]{0,1:T(8,128)S(1)}, f32[256,384]{0,1:T(8,128)}, u32[]{:S(2)}) copy-start(f32[256,384]{0,1:T(8,128)} %copy.44) | copy-start | bytes 1179652
  117.4 2.9 copy-start.33
  117.4 222.5 %all-reduce.10.cloned.1.call-start = ((), (), s32[]{:S(2)}) async-start(), calls=%async_computation | async-start | bytes 7077888 | tf_op jit(solution)/shard_map/psum | solution.py:10
  121.5 6.2 %collective-permute-start.8 = (f32[6,1,32,128]{3,2,1,0:T(8,128)S(1)}, f32[6,1,32,128]{3,2,1,0:T(8,128)S(1)}, u32[]{:S(2)}, u32[]{:S(2)}) collective-permute-start(f32[6,1,32,128]{3,2,1,0:T(8,128)S(1)} %get-tuple-element.178), channel_id=1, source_target_pairs={{1,0},{2,1},{3,2},{5,4},{6,5},{7,6},{9,8},{10,9},{11,10},{13,12},{... | collective-permute-start | bytes 294920 | tf_op jit(solution)/shard_map/ppermute | solution.py:29
  122.8 5.2 %collective-permute-start.7 = (f32[6,1,32,128]{3,2,1,0:T(8,128)S(1)}, f32[6,1,32,128]{3,2,1,0:T(8,128)S(1)}, u32[]{:S(2)}, u32[]{:S(2)}) collective-permute-start(f32[6,1,32,128]{3,2,1,0:T(8,128)S(1)} %get-tuple-element.177), channel_id=1, source_target_pairs={{0,1},{1,2},{2,3},{4,5},{5,6},{6,7},{8,9},{9,10},{10,11},{12,13},{... | collective-permute-start | bytes 294920 | tf_op jit(solution)/shard_map/ppermute | solution.py:27
  339.8 3.0 copy-start.4
  (57 other events, 94.8 us)
Sparse Core Ops, SparseCore 0:
  117.5 79.8 all-reduce.11
  201.0 138.8 all-reduce.9
